TPU v7x, 32 devices: a whole 2x2x4 slice. The times are simulated.
32 devices in a mesh: phase: 2 (over core), tok: 4 (over z), mp: 4 (over y, x).
Axes of the slice: x: 2, y: 2, z: 4, core: 2. Of those that a mesh axis runs over, the one named last changes fastest.
Arguments:
- hidden: bfloat16 [2, 512, 6656], P('phase', 'tok', 'mp'), may hold values from -30 to 30
- w_qkv: bfloat16 [2, 6656, 3, 4096], P('phase', 'mp', None, 'tok'), may hold values from -1 to 1
- segment_ids: int32 [2, 512], P('phase'), may hold values from 0 to 3, never falling along the last dimension, each value on 1 to 256 neighbouring positions
- exit_flags: int32 [2, 4], P('phase'), may hold values from 0 to 1, as said below
Outputs:
- attended: bfloat16 [2, 512, 4096], P('phase', 'mp', 'tok')
- handed: bfloat16 [2, 512, 4096], P('phase', 'mp', 'tok')
Inputs may be any that keep to these rules, and one draw needn't show every extreme that they name: `exit_flags`: in each micro-batch exactly 2 of the 4 blocks have flag 0.
All inputs are finite; a program needn't handle non-finite values.
Results may differ from a plain program's by a relative error of at most 0.0068.
Values may be sent and summed in bfloat16 or wider, within the bound.
A program may use at most 64 MiB of HBM per device.

v0:
```python
import math
import jax
import jax.numpy as jnp
from jax import lax
from jax.sharding import PartitionSpec as P

HEAD = 128
BLOCK = 128


def shifted(block, axis, distance):
    devices = range(lax.axis_size(axis))
    route = [((i - distance) % len(devices), i) for i in devices]
    return lax.ppermute(block, axis, route)


def attend(query, keys, values, query_pos, segment, key_pos):
    heads_here = query.shape[1] // HEAD
    total = keys.shape[0]
    key_heads = keys.reshape(total, heads_here, HEAD)
    value_heads = values.reshape(total, heads_here, HEAD)
    key_segment = jnp.take(segment, key_pos)
    scale = 1.0 / math.sqrt(HEAD)
    block_rows = query.shape[0]
    scores = (
        jnp.einsum(
            "rhd,shd->hrs",
            query.reshape(block_rows, heads_here, HEAD),
            key_heads,
            preferred_element_type=jnp.float32,
        )
        * scale
    )
    own_segment = jnp.take(segment, query_pos)
    allowed = (key_pos[None, :] <= query_pos[:, None]) & (
        key_segment[None, :] == own_segment[:, None]
    )
    scores = jnp.where(allowed[None], scores, -1e30)
    peak = jnp.max(scores, axis=-1, keepdims=True)
    expo = jnp.exp(scores - peak)
    probs = (expo / jnp.sum(expo, axis=-1, keepdims=True)).astype(jnp.bfloat16)
    mixed = jnp.einsum("hrs,shd->rhd", probs, value_heads, preferred_element_type=jnp.float32)
    return mixed.reshape(block_rows, heads_here * HEAD).astype(jnp.bfloat16)


def local(hidden, w_qkv, segment_ids, exit_flags):
    rows_here = hidden[0]
    weights = w_qkv[0]
    width_here = rows_here.shape[1]
    head_cols = weights.shape[2]
    flat_weights = weights.reshape(width_here, 3 * head_cols)
    segment = segment_ids[0]
    flags = exit_flags[0]
    groups = lax.axis_size("mp")
    member = lax.axis_index("mp")
    partial_value = jnp.dot(
        lax.all_gather(rows_here, "tok", axis=0, tiled=True),
        flat_weights,
        preferred_element_type=jnp.float32,
    )
    total = partial_value.shape[0]
    quarter = total // groups
    query_part = partial_value[:, :head_cols]
    key_value_part = partial_value[:, head_cols:]
    my_pos = member * quarter + jnp.arange(quarter, dtype=jnp.int32)
    my_blocks = my_pos // BLOCK
    alive = jnp.take(flags, my_blocks) == 0
    query = lax.psum_scatter(query_part, "mp", scatter_dimension=0, tiled=True).astype(jnp.bfloat16)
    mine = lax.psum_scatter(key_value_part, "mp", scatter_dimension=0, tiled=True).astype(
        jnp.bfloat16
    )
    key_value = lax.all_gather(mine, "mp", axis=0, tiled=True)
    all_pos = jnp.arange(total, dtype=jnp.int32)
    mixed = attend(
        query, key_value[:, :head_cols], key_value[:, head_cols:], my_pos, segment, all_pos
    )
    zeros = jnp.zeros((quarter, head_cols), jnp.bfloat16)
    result = jnp.where(alive[:, None], mixed, zeros)
    handed = shifted(result, "phase", 1)
    return (result[None], handed[None])


def solution(mesh):
    in_specs = (
        P("phase", "tok", "mp"),
        P("phase", "mp", None, "tok"),
        P("phase", None),
        P("phase", None),
    )
    out_specs = (P("phase", "mp", "tok"), P("phase", "mp", "tok"))
    return jax.shard_map(local, mesh=mesh, in_specs=in_specs, out_specs=out_specs, check_vma=False)
```

profile of v0, /device:TPU:0, one launch (start us, length us, event | category | flops | bytes accessed | tf_op | source)
XLA Modules:
  0.0 207.5 jit_solution(11496909522336261351)
XLA Ops:
  7.2 0.0 all-gather.6.cloned.1.call-start
  7.2 0.7 all-gather.6.cloned.1.call-update
  7.9 0.0 reduce-scatter.3.cloned.1.call-start
  8.0 13.5 %copy.11 = bf16[1,1664,3,1024]{1,3,2,0:T(8,128)(2,1)} copy(bf16[1,1664,3,1024]{3,1,2,0:T(8,128)(2,1)} %param.5) | data formatting | bytes 20447232 | tf_op args[1]
  21.5 30.0 %all-gather.6.cloned.1.call-done = bf16[1,512,1664]{2,1,0:T(8,128)(2,1)} async-done(((bf16[1,128,1664]{2,1,0:T(8,128)(2,1)}), bf16[1,512,1664]{2,1,0:T(8,128)(2,1)}) %all-gather.6.cloned.1.call-update) | async-done | bytes 1703952 | tf_op jit(solution)/shard_map/all_gather | solution.py:57
  51.5 9.1 %fusion.2 = f32[512,3072]{1,0:T(8,128)S(1)} fusion(bf16[1664,3072]{0,1:T(8,128)(2,1)} %bitcast.57, bf16[1,512,1664]{2,1,0:T(8,128)(2,1)} %all-gather.6.cloned.1.call-done), kind=kOutput, calls=%fused_computation.7 | convolution fusion | flops 5234491392 | bytes 18219008 | tf_op jit(solution)/shard_map/dot_general | solution.py:56
  60.6 2.7 %copy-done.1 = f32[512,3072]{1,0:T(8,128)} copy-done((f32[512,3072]{1,0:T(8,128)}, f32[512,3072]{1,0:T(8,128)S(1)}, u32[]{:S(2)}) %copy-start.1) | copy-done | bytes 6291480
  63.3 2.5 %slice.30 = f32[512,2048]{1,0:T(8,128)} slice(f32[512,3072]{1,0:T(8,128)S(1)} %fusion.2), slice={[0:512], [1024:3072]} | slice | bytes 8388608 | tf_op jit(solution)/shard_map/slice | solution.py:64
  65.8 0.0 reduce-scatter.3.cloned.1.call-update
  65.8 0.0 all-gather.4.cloned.1.call-start
  65.9 51.5 %reduce-scatter.3.cloned.1.call-done = f32[128,2048]{1,0:T(8,128)} async-done(((f32[512,2048]{1,0:T(8,128)}), f32[128,2048]{1,0:T(8,128)}) %reduce-scatter.3.cloned.1.call-update) | async-done | bytes 1048592 | tf_op jit(solution)/shard_map/reduce_scatter | solution.py:69
  117.4 2.1 %convert_element_type.29 = bf16[128,2048]{1,0:T(8,128)(2,1)} convert(f32[128,2048]{1,0:T(8,128)} %reduce-scatter.3.cloned.1.call-done) | non-fusion elementwise | flops 262144 | bytes 1572864 | tf_op jit(solution)/shard_map/convert_element_type | solution.py:69
  119.5 0.0 reduce-scatter.5.cloned.1.call-start
  119.6 3.2 %slice.32 = f32[512,1024]{1,0:T(8,128)} slice(f32[512,3072]{1,0:T(8,128)} %copy-done.1), slice={[0:512], [0:1024]} | slice | bytes 4194304 | tf_op jit(solution)/shard_map/slice | solution.py:63
  122.8 3.5 %gather_fusion = s32[512]{0:T(512)S(1)} fusion(s32[512]{0:T(512)S(1)} %bitcast.55, s32[1024]{0:T(1024)S(1)} %pad_clamp_fusion.1), kind=kCustom, calls=%fused_computation | custom fusion | bytes 6144 | tf_op jit(solution)/shard_map/jit(_take)/gather | solution.py:22
  126.4 1.3 gather_fusion.1
  127.7 0.7 fusion.31
  128.3 2.6 %fusion.28 = pred[128]{0:T(512)(128)(4,1)S(1)} fusion(s32[]{:T(128)} %bitcast, s32[]{:T(128)} %bitcast.1, s32[]{:T(128)} %bitcast.3, s32[]{:T(128)} %bitcast.2, s32[]{:T(128)S(6)} %mul.9), kind=kLoop, calls=%fused_computation.48 | loop fusion | flops 6272 | bytes 148 | tf_op jit(solution)/shard_map/eq | solution.py:67
  130.9 0.1 fusion.12
  131.0 23.8 %all-gather.4.cloned.1.call-done = bf16[512,2048]{1,0:T(8,128)(2,1)} async-done(((bf16[128,2048]{1,0:T(8,128)(2,1)}), bf16[512,2048]{1,0:T(8,128)(2,1)}) %all-gather.4.cloned.1.call-update) | async-done | bytes 2097168 | tf_op jit(solution)/shard_map/all_gather | solution.py:72
  154.9 1.7 slice_bitcast_fusion
  156.6 0.5 copy.17
  157.2 35.7 %reduce-scatter.5.cloned.1.call-done = f32[128,1024]{1,0:T(8,128)} async-done(((f32[512,1024]{1,0:T(8,128)}), f32[128,1024]{1,0:T(8,128)}) %reduce-scatter.5.cloned.1.call-update) | async-done | bytes 524304 | tf_op jit(solution)/shard_map/reduce_scatter | solution.py:68
  192.9 3.3 %fusion.32 = (f32[8,128]{1,0:T(8,128)S(1)}, f32[8,128,512]{2,1,0:T(8,128)}) fusion(pred[128,512]{1,0:T(8,128)(4,1)S(1)} %fusion.12, bf16[64,8,8,128]{3,2,1,0:T(8,128)(2,1)S(1)} %get-tuple-element.2, f32[128,1024]{1,0:T(8,128)} %reduce-scatter.5.cloned.1.call-done), kind=kOutput, calls=%fused_computation.53 | convolution fusion | flops 136446464 | bytes 3739648 | tf_op jit(solution)/shard_map/sub | solution.py:40
  196.2 2.2 %convolution_convert_fusion = bf16[8,128,128]{2,1,0:T(8,128)(2,1)S(1)} fusion(bf16[512,8,128]{0,2,1:T(8,128)(2,1)S(1)} %bitcast.58, f32[8,128,512]{2,1,0:T(8,128)} %get-tuple-element.9, f32[8,128]{1,0:T(8,128)S(1)} %get-tuple-element.8), kind=kOutput, calls=%fused_computation.9 | convolution fusion | flops 135397376 | bytes 3411968 | tf_op jit(solution)/shard_map/hrs,shd->rhd/dot_general | solution.py:42
  198.4 0.1 copy.16
  198.6 0.1 broadcast_select_fusion
  198.6 0.1 collective-permute-start
  198.7 0.1 copy.15
  198.9 0.8 broadcast_select_fusion.1
  199.7 0.6 collective-permute-done
  200.2 0.7 copy.45
  (13 shorter events, 0.1 us)
Async XLA Ops:
  7.2 115.7 %copy-start = (s32[1,512]{1,0:T(1,128)S(1)}, s32[1,512]{1,0:T(1,128)}, u32[]{:S(2)}) copy-start(s32[1,512]{1,0:T(1,128)} %param.6) | copy-start | bytes 6148
  7.2 44.3 %all-gather.6.cloned.1.call-start = ((), (), s32[]{:S(2)}) async-start(), calls=%async_computation.5 | async-start | bytes 2129920 | tf_op jit(solution)/shard_map/all_gather | solution.py:57
  7.9 109.5 %reduce-scatter.3.cloned.1.call-start = ((), (), s32[]{:S(2)}) async-start(), calls=%async_computation.2 | async-start | bytes 5242880 | tf_op jit(solution)/shard_map/reduce_scatter | solution.py:69
  60.6 2.7 %copy-start.1 = (f32[512,3072]{1,0:T(8,128)}, f32[512,3072]{1,0:T(8,128)S(1)}, u32[]{:S(2)}) copy-start(f32[512,3072]{1,0:T(8,128)S(1)} %fusion.2) | copy-start | bytes 18874372
  65.8 89.1 %all-gather.4.cloned.1.call-start = ((), (), s32[]{:S(2)}) async-start(), calls=%async_computation.3 | async-start | bytes 2621440 | tf_op jit(solution)/shard_map/all_gather | solution.py:72
  119.5 73.4 %reduce-scatter.5.cloned.1.call-start = ((), (), s32[]{:S(2)}) async-start(), calls=%async_computation.4 | async-start | bytes 2621440 | tf_op jit(solution)/shard_map/reduce_scatter | solution.py:68
  122.8 4.9 %copy-start.2 = (s32[1,4]{1,0:T(1,128)S(1)}, s32[1,4]{1,0:T(1,128)}, u32[]{:S(2)}) copy-start(s32[1,4]{1,0:T(1,128)} %param.7) | copy-start | bytes 52
  198.6 1.6 collective-permute-start
Sparse Core Ops, SparseCore 0:
  9.6 41.8 all-gather.5
  65.9 51.4 reduce-scatter.2
  119.6 35.1 all-gather.3
  157.7 35.1 reduce-scatter.4
where the time goes:
time: 208 us; the launch traced here: 207 us
  waiting for transfers between devices  142 us (68%)
  local copies, waits for them, and re-layouts  30.7 us (15%)
  matrix products  14.6 us (7%)
  between operations  13.9 us (7%)
  other arithmetic  5.68 us (3%)
    reduce_scatter x1, waiting for transfers between devices, local(): lax.psum_scatter(key_value_part, 'mp', scatter_dimension=0, tiled=True)  51.5 us
    reduce_scatter x1, waiting for transfers between devices, local(): lax.psum_scatter(query_part, 'mp', scatter_dimension=0, tiled=True)  35.7 us
    all_gather x1, waiting for transfers between devices, local(): lax.all_gather(rows_here, 'tok', axis=0, tiled=True)  30 us
    all_gather x1, waiting for transfers between devices, local(): key_value = lax.all_gather(mine, 'mp', axis=0, tiled=True)  23.8 us
    unnamed x9, local copies, waits for them, and re-layouts  18.7 us
    dot_general x1, matrix products, local(): jnp.dot(lax.all_gather(rows_here, 'tok', axis=0, tiled=True), flat_weight...  9.08 us
  transfers between devices with their start and end apart: 5, of which 5 were waited for; matrix products, arithmetic and copies ran while one was open for 14% of the time, Pallas kernels for 0%

commit v1 on v0

--- a/solution.py
+++ b/solution.py
@@ -6,6 +6,23 @@
 
 HEAD = 128
 BLOCK = 128
+
+
+def laid_out(tiles, dim):
+    tiles = jnp.moveaxis(tiles, 0, dim)
+    lengths = tiles.shape
+    return tiles.reshape(*lengths[:dim], lengths[dim] * lengths[dim + 1], *lengths[dim + 2 :])
+
+
+def doubled(array, axis):
+    size, position = (lax.axis_size(axis), lax.axis_index(axis))
+    tiles, bit = (array[None], 1)
+    while bit < size:
+        theirs = lax.ppermute(tiles, axis, [(i, i ^ bit) for i in range(size)])
+        low = position & bit == 0
+        tiles = jnp.concatenate([jnp.where(low, tiles, theirs), jnp.where(low, theirs, tiles)])
+        bit *= 2
+    return tiles
 
 
 def shifted(block, axis, distance):
@@ -69,7 +86,7 @@
     mine = lax.psum_scatter(key_value_part, "mp", scatter_dimension=0, tiled=True).astype(
         jnp.bfloat16
     )
-    key_value = lax.all_gather(mine, "mp", axis=0, tiled=True)
+    key_value = laid_out(doubled(mine, "mp"), 0)
     all_pos = jnp.arange(total, dtype=jnp.int32)
     mixed = attend(
         query, key_value[:, :head_cols], key_value[:, head_cols:], my_pos, segment, all_pos

time: 208 us -> 185 us (0.89)
  waiting for transfers between devices: 142 us -> 118 us
  starting transfers between devices: 0.23 us -> 3.08 us
    ppermute x0 -> x2, waiting for transfers between devices: none -> 38.5 us  [doubled(): theirs = lax.ppermute(tiles, axis, [(i, i ^ bit) for i in range(size)])]
    reduce_scatter x1, waiting for transfers between devices: 35.7 us -> 0.02 us  [local(): lax.psum_scatter(query_part, 'mp', scatter_dimension=0, tiled=True)]
    all_gather x1 -> x0, waiting for transfers between devices: 23.8 us -> none  [local(): key_value = lax.all_gather(mine, 'mp', axis=0, tiled=True)]
    reduce_scatter x1, waiting for transfers between devices: 51.5 us -> 48.3 us  [local(): lax.psum_scatter(key_value_part, 'mp', scatter_dimension=0, tiled=True)]
    ppermute x0 -> x2, starting transfers between devices: none -> 2.89 us  [doubled(): theirs = lax.ppermute(tiles, axis, [(i, i ^ bit) for i in range(size)])]
    convert_element_type x1 -> x0, other arithmetic: 2.09 us -> none  [local(): lax.psum_scatter(key_value_part, 'mp', scatter_dimension=0, tiled=True)]
    unnamed x9 -> x11, local copies, waits for them, and re-layouts: 18.7 us -> 17.2 us
  transfers between devices with their start and end apart: 5 -> 6, of which waited for: 5 -> 5; matrix products, arithmetic and copies ran while one was open for 14% -> 16% of each run, Pallas kernels for 0% -> 0%
where the time goes in v1:
time: 185 us
  waiting for transfers between devices  118 us (64%)
  local copies, waits for them, and re-layouts  29.3 us (16%)
  matrix products  14.5 us (8%)
  between operations  14 us (8%)
  other arithmetic  5.49 us (3%)
  starting transfers between devices  3.08 us (2%)
    reduce_scatter x1, waiting for transfers between devices, local(): lax.psum_scatter(key_value_part, 'mp', scatter_dimension=0, tiled=True)  48.3 us
    ppermute x2, waiting for transfers between devices, doubled(): theirs = lax.ppermute(tiles, axis, [(i, i ^ bit) for i in range(size)])  38.5 us
    all_gather x1, waiting for transfers between devices, local(): lax.all_gather(rows_here, 'tok', axis=0, tiled=True)  30.2 us
    unnamed x11, local copies, waits for them, and re-layouts  17.2 us
    dot_general x1, matrix products, local(): jnp.dot(lax.all_gather(rows_here, 'tok', axis=0, tiled=True), flat_weight...  9.08 us
  transfers between devices with their start and end apart: 6, of which 5 were waited for; matrix products, arithmetic and copies ran while one was open for 16% of the time, Pallas kernels for 0%

profile of v1, /device:TPU:0, one launch (start us, length us, event | category | flops | bytes accessed | tf_op | source)
XLA Modules:
  0.0 184.8 jit_solution(17251621786394190999)
XLA Ops:
  7.2 0.7 all-gather.3.cloned.1.call-update
  8.0 13.3 %copy.10 = bf16[1,1664,3,1024]{1,3,2,0:T(8,128)(2,1)} copy(bf16[1,1664,3,1024]{3,1,2,0:T(8,128)(2,1)} %param.5) | data formatting | bytes 20447232 | tf_op args[1]
  21.2 30.2 %all-gather.3.cloned.1.call-done = bf16[1,512,1664]{2,1,0:T(8,128)(2,1)} async-done(((bf16[1,128,1664]{2,1,0:T(8,128)(2,1)}), bf16[1,512,1664]{2,1,0:T(8,128)(2,1)}) %all-gather.3.cloned.1.call-update) | async-done | bytes 1703952 | tf_op jit(solution)/shard_map/all_gather | solution.py:74
  51.5 9.1 %fusion.2 = f32[512,3072]{1,0:T(8,128)S(1)} fusion(bf16[1664,3072]{0,1:T(8,128)(2,1)} %bitcast.51, bf16[1,512,1664]{2,1,0:T(8,128)(2,1)} %all-gather.3.cloned.1.call-done), kind=kOutput, calls=%fused_computation.8 | convolution fusion | flops 5234491392 | bytes 18219008 | tf_op jit(solution)/shard_map/dot_general | solution.py:73
  60.6 2.7 %copy-done.1 = f32[512,3072]{1,0:T(8,128)} copy-done((f32[512,3072]{1,0:T(8,128)}, f32[512,3072]{1,0:T(8,128)S(1)}, u32[]{:S(2)}) %copy-start.1) | copy-done | bytes 6291480
  63.2 2.5 %slice.30 = f32[512,2048]{1,0:T(8,128)} slice(f32[512,3072]{1,0:T(8,128)S(1)} %fusion.2), slice={[0:512], [1024:3072]} | slice | bytes 8388608 | tf_op jit(solution)/shard_map/slice | solution.py:81
  65.8 3.2 %slice.32 = f32[512,1024]{1,0:T(8,128)} slice(f32[512,3072]{1,0:T(8,128)} %copy-done.1), slice={[0:512], [0:1024]} | slice | bytes 4194304 | tf_op jit(solution)/shard_map/slice | solution.py:80
  69.0 48.3 %reduce-scatter.3.cloned.1.call-done = f32[128,2048]{1,0:T(8,128)} async-done(((f32[512,2048]{1,0:T(8,128)}), f32[128,2048]{1,0:T(8,128)}) %reduce-scatter.3.cloned.1.call-update) | async-done | bytes 1048592 | tf_op jit(solution)/shard_map/reduce_scatter | solution.py:86
  117.4 1.4 convert_bitcast_fusion
  118.8 1.5 collective-permute-start
  120.3 16.9 %collective-permute-done = bf16[1,128,2048]{2,1,0:T(8,128)(2,1)S(1)} collective-permute-done((bf16[1,128,2048]{2,1,0:T(8,128)(2,1)S(1)}, bf16[1,128,2048]{2,1,0:T(8,128)(2,1)S(1)}, u32[]{:S(2)}, u32[]{:S(2)}) %collective-permute-start) | collective-permute-done | bytes 524320 | tf_op jit(solution)/shard_map/ppermute | solution.py:21
  137.2 0.1 broadcast_select_fusion.3
  137.3 0.1 pad_maximum_fusion.1
  137.4 1.4 collective-permute-start.1
  138.7 1.3 gather_fusion.1
  140.0 3.5 %gather_fusion = s32[512]{0:T(512)S(1)} fusion(s32[512]{0:T(512)S(1)} %bitcast.49, s32[1024]{0:T(1024)S(1)} %pad_clamp_fusion.1), kind=kCustom, calls=%fused_computation | custom fusion | bytes 6144 | tf_op jit(solution)/shard_map/jit(_take)/gather | solution.py:39
  143.6 0.6 fusion.24
  144.2 2.6 %fusion.20 = pred[128]{0:T(512)(128)(4,1)S(1)} fusion(s32[]{:T(128)} %bitcast, s32[]{:T(128)} %bitcast.1, s32[]{:T(128)} %bitcast.3, s32[]{:T(128)} %bitcast.2, s32[]{:T(128)S(6)} %mul.9), kind=kLoop, calls=%fused_computation.52 | loop fusion | flops 6272 | bytes 148 | tf_op jit(solution)/shard_map/eq | solution.py:84
  146.8 0.1 fusion.10
  146.9 21.7 %collective-permute-done.1 = bf16[2,128,2048]{2,1,0:T(8,128)(2,1)S(1)} collective-permute-done((bf16[2,128,2048]{2,1,0:T(8,128)(2,1)S(1)}, bf16[2,128,2048]{2,1,0:T(8,128)(2,1)S(1)}, u32[]{:S(2)}, u32[]{:S(2)}) %collective-permute-start.1) | collective-permute-done | bytes 1048608 | tf_op jit(solution)/shard_map/ppermute | solution.py:21
  168.6 0.1 broadcast_select_fusion.1
  168.7 0.2 pad_maximum_fusion
  168.9 0.2 fusion.23
  169.1 0.5 copy.18
  169.7 0.5 copy.11
  170.3 3.2 %fusion.25 = (f32[8,128]{1,0:T(8,128)S(1)}, f32[8,128,512]{2,1,0:T(8,128)}) fusion(pred[128,512]{1,0:T(8,128)(4,1)S(1)} %fusion.10, bf16[512,8,128]{0,2,1:T(8,128)(2,1)S(1)} %bitcast.53, f32[128,1024]{1,0:T(8,128)} %reduce-scatter.5.cloned.1.call-done), kind=kOutput, calls=%fused_computation.58 | convolution fusion | flops 136446464 | bytes 3739648 | tf_op jit(solution)/shard_map/sub | solution.py:57
  173.5 2.2 %convolution_convert_fusion = bf16[8,128,128]{2,1,0:T(8,128)(2,1)S(1)} fusion(bf16[512,8,128]{0,2,1:T(8,128)(2,1)S(1)} %bitcast.54, f32[8,128,512]{2,1,0:T(8,128)} %get-tuple-element.13, f32[8,128]{1,0:T(8,128)S(1)} %get-tuple-element.12), kind=kOutput, calls=%fused_computation.10 | convolution fusion | flops 135397376 | bytes 3411968 | tf_op jit(solution)/shard_map/hrs,shd->rhd/dot_general | solution.py:59
  175.7 0.1 copy.16
  176.0 0.1 copy.15
  176.2 0.8 broadcast_select_fusion.5
  177.0 0.6 collective-permute-done.2
  177.5 0.7 copy.33
  (21 shorter events, 0.4 us)
Async XLA Ops:
  7.2 131.6 %copy-start = (s32[1,512]{1,0:T(1,128)S(1)}, s32[1,512]{1,0:T(1,128)}, u32[]{:S(2)}) copy-start(s32[1,512]{1,0:T(1,128)} %param.6) | copy-start | bytes 6148
  7.2 44.3 %all-gather.3.cloned.1.call-start = ((), (), s32[]{:S(2)}) async-start(), calls=%async_computation.4 | async-start | bytes 2129920 | tf_op jit(solution)/shard_map/all_gather | solution.py:74
  7.9 109.5 %reduce-scatter.3.cloned.1.call-start = ((), (), s32[]{:S(2)}) async-start(), calls=%async_computation.2 | async-start | bytes 5242880 | tf_op jit(solution)/shard_map/reduce_scatter | solution.py:86
  60.6 2.7 %copy-start.1 = (f32[512,3072]{1,0:T(8,128)}, f32[512,3072]{1,0:T(8,128)S(1)}, u32[]{:S(2)}) copy-start(f32[512,3072]{1,0:T(8,128)S(1)} %fusion.2) | copy-start | bytes 18874372
  65.8 104.5 %reduce-scatter.5.cloned.1.call-start = ((), (), s32[]{:S(2)}) async-start(), calls=%async_computation.3 | async-start | bytes 2621440 | tf_op jit(solution)/shard_map/reduce_scatter | solution.py:85
  117.4 19.8 %copy-start.2 = (f32[128,2048]{1,0:T(8,128)S(1)}, f32[128,2048]{1,0:T(8,128)}, u32[]{:S(2)}) copy-start(f32[128,2048]{1,0:T(8,128)} %reduce-scatter.3.cloned.1.call-done) | copy-start | bytes 3145732
  118.8 18.4 %collective-permute-start = (bf16[1,128,2048]{2,1,0:T(8,128)(2,1)S(1)}, bf16[1,128,2048]{2,1,0:T(8,128)(2,1)S(1)}, u32[]{:S(2)}, u32[]{:S(2)}) collective-permute-start(bf16[1,128,2048]{2,1,0:T(8,128)(2,1)S(1)} %convert_bitcast_fusion), channel_id=1, source_target_pairs={{0,1},{1,0},{2,3},{3,2},{4,5},{5,4},{6,7},{7,6},{8,9},{9,8},{10,11... | collective-permute-start | bytes 1572872 | tf_op jit(solution)/shard_map/ppermute | solution.py:21
  137.3 6.3 %copy-start.3 = (s32[1,4]{1,0:T(1,128)S(1)}, s32[1,4]{1,0:T(1,128)}, u32[]{:S(2)}) copy-start(s32[1,4]{1,0:T(1,128)} %param.7) | copy-start | bytes 52
  137.4 31.2 %collective-permute-start.1 = (bf16[2,128,2048]{2,1,0:T(8,128)(2,1)S(1)}, bf16[2,128,2048]{2,1,0:T(8,128)(2,1)S(1)}, u32[]{:S(2)}, u32[]{:S(2)}) collective-permute-start(bf16[2,128,2048]{2,1,0:T(8,128)(2,1)S(1)} %pad_maximum_fusion.1), channel_id=1, source_target_pairs={{0,2},{1,3},{2,0},{3,1},{4,6},{5,7},{6,4},{7,5},{8,10},{9,11},{10,... | collective-permute-start | bytes 3145736 | tf_op jit(solution)/shard_map/ppermute | solution.py:21
  175.9 1.6 collective-permute-start.2
Sparse Core Ops, SparseCore 0:
  9.6 41.8 all-gather.2
  65.9 51.4 reduce-scatter.2
  120.3 45.0 reduce-scatter.4
